TPU v7x, 32 devices: a whole 2x2x4 slice. The times are simulated.
32 devices in a mesh: groups: 2 (over y), frames: 4 (over z), fsdp: 2 (over x), heads: 2 (over core).
Axes of the slice: x: 2, y: 2, z: 4, core: 2. Of those that a mesh axis runs over, the one named last changes fastest.
Arguments:
- frames_in: bfloat16 [4, 768, 1536], P(('groups', 'fsdp'), 'frames', 'heads'), parts along dimension 0, may hold values from -6 to 6
- lengths: int32 [4], P(('groups', 'fsdp')), parts along dimension 0, may hold values from 192 to 768, as said below
- w_query: bfloat16 [1536, 768], P(('frames', 'fsdp'), 'heads')
- w_key: bfloat16 [1536, 768], P(('frames', 'fsdp'), 'heads'), may hold values from -0.15625 to 0.15625
- w_value: bfloat16 [1536, 768], P(('frames', 'fsdp'), 'heads'), may hold values from -0.15625 to 0.15625
- w_out: bfloat16 [768, 1536], P('heads', ('frames', 'fsdp')), may hold values from -0.21875 to 0.21875
- w_glu: bfloat16 [1536, 2, 1536], P('fsdp', None, 'heads'), may hold values from -0.15625 to 0.15625
- dw_kernel: bfloat16 [31, 1536], P(None, 'heads'), may hold values from -1 to 1
- w_pw: bfloat16 [1536, 1536], P('heads', 'fsdp'), may hold values from -0.15625 to 0.15625
Outputs:
- block_out: bfloat16 [4, 768, 1536], P(('groups', 'fsdp'), 'frames', 'heads'), parts along dimension 0
There are 2 independent parts, one for each index of `groups`. A program takes and returns all parts, laid end to end along the dimension named above; an argument that names none is the same for every part. Nothing has to cross between parts.
Inputs may be any that keep to these rules, and one draw needn't show every extreme that they name: `lengths`: each utterance counts at least 192 valid frames, and in every group some utterance is valid over all 768 frames.
All inputs are finite; a program needn't handle non-finite values.
Results may differ from a plain program's by a relative error of at most 0.012.
The roundings to bfloat16 on the way count: a program that leaves them out, or rounds other values in their place, can miss the bound.
Values may be sent and summed in bfloat16 or wider, within the bound.
No kernel may reach another device: no remote copies, remote signals or barrier semaphores. Data moves between devices by JAX's collectives and lax.ppermute only.
A program may use at most 64 MiB of HBM per device.

v0:
```python
import math

import jax
import jax.numpy as jnp
from jax import lax
from jax.sharding import PartitionSpec as P

HEAD_DIM = 96
KERNEL = 31


EPS = 1e-05
NEG_FILL = -1e30


def padded_2(cells, sides, width):
    for axis, dim in sides:
        count = lax.axis_size(axis)
        ends = count - 1
        head = lax.slice_in_dim(cells, 0, width, axis=dim)
        tail = lax.slice_in_dim(cells, cells.shape[dim] - width, cells.shape[dim], axis=dim)
        cells = jnp.concatenate(
            [
                lax.ppermute(tail, axis, [(i, (i + 1) % count) for i in range(ends)]),
                cells,
                lax.ppermute(head, axis, [((i + 1) % count, i) for i in range(ends)]),
            ],
            axis=dim,
        )
    return cells


def layer_norm(rows):
    values = rows.astype(jnp.float32)
    mean_row = jnp.mean(values, axis=-1, keepdims=True)
    centred = values - mean_row
    variance = jnp.mean(centred * centred, axis=-1, keepdims=True)
    return centred * lax.rsqrt(variance + EPS)


def shards(frames_in, lengths, w_query, w_key, w_value, w_out, w_glu, dw_kernel, w_pw):
    full_rows = lax.all_gather(frames_in, "heads", axis=2, tiled=True)[0]
    frame_count = full_rows.shape[0]
    half_width = frames_in.shape[2]
    own_start = lax.axis_index("heads") * half_width
    normed = layer_norm(full_rows).astype(jnp.bfloat16)
    att_cols = w_query.shape[1]
    pieces = (
        lax.all_gather(w_query, ("frames", "fsdp"), axis=0, tiled=True),
        lax.all_gather(w_key, ("frames", "fsdp"), axis=0, tiled=True),
        lax.all_gather(w_value, ("frames", "fsdp"), axis=0, tiled=True),
    )
    sliced = normed
    projected = tuple(
        (jnp.dot(sliced, piece_part, preferred_element_type=jnp.float32) for piece_part in pieces)
    )
    head_count = att_cols // HEAD_DIM
    queries = projected[0].astype(jnp.bfloat16).reshape(frame_count, head_count, HEAD_DIM)
    key_rows = projected[1].astype(jnp.bfloat16)
    value_rows = projected[2].astype(jnp.bfloat16)
    length = lengths[0]
    scale_factor = 1.0 / math.sqrt(HEAD_DIM)
    start_max = jnp.full((frame_count, head_count), NEG_FILL, jnp.float32)
    pieces = (
        lax.all_gather(key_rows, "frames", axis=0, tiled=True),
        lax.all_gather(value_rows, "frames", axis=0, tiled=True),
    )
    key_block = pieces[0].reshape(-1, head_count, HEAD_DIM)
    value_block = pieces[1].reshape(-1, head_count, HEAD_DIM)
    block_rows = key_block.shape[0]
    scores = (
        jnp.einsum("qhd,khd->qhk", queries, key_block, preferred_element_type=jnp.float32)
        * scale_factor
    )
    valid = jnp.arange(block_rows, dtype=jnp.int32) < length
    masked = jnp.where(valid, scores, NEG_FILL)
    new_max = jnp.maximum(start_max, jnp.max(masked, axis=2))
    expo = jnp.where(valid, jnp.exp(masked - new_max[:, :, None]), 0.0)
    new_sum = jnp.sum(expo, axis=2)
    block_acc = jnp.einsum(
        "qhk,khd->qhd", expo.astype(jnp.bfloat16), value_block, preferred_element_type=jnp.float32
    )
    context = (block_acc / new_sum[:, :, None]).reshape(frame_count, att_cols).astype(jnp.bfloat16)
    partial_value = jnp.dot(
        context,
        lax.all_gather(w_out, ("frames", "fsdp"), axis=1, tiled=True),
        preferred_element_type=jnp.float32,
    )
    total = lax.psum(partial_value.astype(jnp.bfloat16), "heads").astype(jnp.float32)
    stream_full = (full_rows.astype(jnp.float32) + total).astype(jnp.bfloat16)
    stream_own = lax.dynamic_slice_in_dim(stream_full, own_start, half_width, 1)
    normed_two = layer_norm(stream_full).astype(jnp.bfloat16)
    channels = w_glu.shape[2]
    sliced = normed_two
    glu_pre = jnp.einsum(
        "td,dgc->tgc",
        sliced,
        lax.all_gather(w_glu, "fsdp", axis=0, tiled=True),
        preferred_element_type=jnp.float32,
    )
    positions = lax.axis_index("frames") * frame_count + jnp.arange(frame_count, dtype=jnp.int32)
    live = positions < length
    gated = jnp.where(
        live[:, None], glu_pre[:, 0, :] * jax.nn.sigmoid(glu_pre[:, 1, :]), 0.0
    ).astype(jnp.bfloat16)
    padded = padded_2(gated, (("frames", 0),), KERNEL // 2)
    depth = jnp.zeros((frame_count, channels), jnp.float32)
    for tap_index in range(KERNEL):
        depth = depth + padded[tap_index : tap_index + frame_count].astype(jnp.float32) * dw_kernel[
            tap_index
        ].astype(jnp.float32)
    hidden = (depth * jax.nn.sigmoid(depth)).astype(jnp.bfloat16)
    conv_part = jnp.dot(
        hidden, lax.all_gather(w_pw, "fsdp", axis=1, tiled=True), preferred_element_type=jnp.float32
    )
    conv_half = lax.psum_scatter(
        conv_part.astype(jnp.bfloat16), "heads", scatter_dimension=1, tiled=True
    ).astype(jnp.float32)
    result = (stream_own.astype(jnp.float32) + conv_half).astype(jnp.bfloat16)
    return result[None]


def solution(mesh):
    in_specs = (
        P(("groups", "fsdp"), "frames", "heads"),
        P(("groups", "fsdp")),
        P(("frames", "fsdp"), "heads"),
        P(("frames", "fsdp"), "heads"),
        P(("frames", "fsdp"), "heads"),
        P("heads", ("frames", "fsdp")),
        P("fsdp", None, "heads"),
        P(None, "heads"),
        P("heads", "fsdp"),
    )
    out_specs = P(("groups", "fsdp"), "frames", "heads")
    return jax.shard_map(shards, mesh=mesh, in_specs=in_specs, out_specs=out_specs, check_vma=False)
```

profile of v0, /device:TPU:0, one launch (start us, length us, event | category | flops | bytes accessed | tf_op | source)
XLA Modules:
  0.0 307.6 jit_solution(13441506892905612474)
XLA Ops:
  10.2 2.6 all_gather.27
  13.9 40.3 %all-gather.9.cloned.1.call-done = bf16[1536,384]{1,0:T(8,128)(2,1)} async-done(((bf16[192,384]{1,0:T(8,128)(2,1)}), bf16[1536,384]{1,0:T(8,128)(2,1)}) %all-gather.9.cloned.1.call-update) | async-done | bytes 1179664 | tf_op jit(solution)/shard_map/all_gather | solution.py:50
  54.2 1.8 convolution_convert_fusion.3
  56.0 18.1 %all_gather.31 = bf16[768,384]{1,0:T(8,128)(2,1)S(1)} all-gather(bf16[192,384]{1,0:T(8,128)(2,1)S(1)} %convolution_convert_fusion.3), channel_id=1, replica_groups=mesh['groups'=2,'frames'=4,'fsdp'=2,'heads'=2] {'frames'}, dimensions={0}, use_global_device_ids=true | all-gather | bytes 737280 | tf_op jit(solution)/shard_map/all_gather | solution.py:65
  74.4 22.4 %all-gather.11.cloned.1.call-done = bf16[1536,384]{1,0:T(8,128)(2,1)} async-done(((bf16[192,384]{1,0:T(8,128)(2,1)}), bf16[1536,384]{1,0:T(8,128)(2,1)}) %all-gather.11.cloned.1.call-update) | async-done | bytes 1179664 | tf_op jit(solution)/shard_map/all_gather | solution.py:49
  96.8 1.8 convolution_convert_fusion.2
  98.7 40.1 %all-gather.7.cloned.1.call-done = bf16[1536,384]{1,0:T(8,128)(2,1)} async-done(((bf16[192,384]{1,0:T(8,128)(2,1)}), bf16[1536,384]{1,0:T(8,128)(2,1)}) %all-gather.7.cloned.1.call-update) | async-done | bytes 1179664 | tf_op jit(solution)/shard_map/all_gather | solution.py:51
  138.8 1.8 convolution_convert_fusion.4
  140.6 18.1 %all_gather.29 = bf16[768,384]{1,0:T(8,128)(2,1)S(1)} all-gather(bf16[192,384]{1,0:T(8,128)(2,1)S(1)} %convolution_convert_fusion.4), channel_id=1, replica_groups=mesh['groups'=2,'frames'=4,'fsdp'=2,'heads'=2] {'frames'}, dimensions={0}, use_global_device_ids=true | all-gather | bytes 737280 | tf_op jit(solution)/shard_map/all_gather | solution.py:66
  159.5 0.7 fusion.2
  160.2 0.8 fusion.22
  161.0 20.3 %all-gather.13.cloned.1.call-done = bf16[384,1536]{0,1:T(8,128)(2,1)} async-done(((bf16[384,192]{0,1:T(8,128)(2,1)}), bf16[384,1536]{0,1:T(8,128)(2,1)}) %all-gather.13.cloned.1.call-update) | async-done | bytes 1179664 | tf_op jit(solution)/shard_map/all_gather | solution.py:86
  181.4 2.8 convolution_convert_fusion.1
  184.3 1.8 copy.17
  187.1 14.7 %all-reduce.2.cloned.1.call-done = bf16[192,1536]{1,0:T(8,128)(2,1)} async-done(((bf16[192,1536]{1,0:T(8,128)(2,1)}), bf16[192,1536]{1,0:T(8,128)(2,1)}) %all-reduce.2.cloned.1.call-update) | async-done | bytes 589840 | tf_op jit(solution)/shard_map/psum | solution.py:89
  201.8 1.3 convert_reduce_fusion
  203.4 44.1 %all-gather.15.cloned.1.call-done = bf16[1536,2,768]{2,0,1:T(8,128)(2,1)} async-done(((bf16[768,2,768]{2,0,1:T(8,128)(2,1)}), bf16[1536,2,768]{2,0,1:T(8,128)(2,1)}) %all-gather.15.cloned.1.call-update) | async-done | bytes 4718608 | tf_op jit(solution)/shard_map/all_gather | solution.py:98
  247.5 3.5 %fusion.26 = f32[192,2,768]{2,0,1:T(8,128)S(1)} fusion(bf16[1536,2,768]{2,0,1:T(8,128)(2,1)} %all-gather.15.cloned.1.call-done, bf16[192,1536]{1,0:T(8,128)(2,1)S(1)} %get-tuple-element.37, f32[192]{0:T(256)S(1)} %add_rsqrt_fusion, f32[192]{0:T(256)S(1)} %broadcast_multiply_fusion), kind=kOutput, calls=%fused_computation.64 | convolution fusion | flops 907149312 | bytes 6489600 | tf_op jit(solution)/shard_map/td,dgc->tgc/dot_general | solution.py:95
  251.2 3.4 %collective-permute-start = (bf16[15,768]{1,0:T(8,128)(2,1)S(1)}, bf16[15,768]{1,0:T(8,128)(2,1)S(1)}, u32[]{:S(2)}, u32[]{:S(2)}) collective-permute-start(bf16[15,768]{1,0:T(8,128)(2,1)S(1)} %get-tuple-element.38), channel_id=1, source_target_pairs={{0,4},{4,8},{8,12},{1,5},{5,9},{9,13},{2,6},{6,10},{10,14},{3,7},{... | collective-permute-start | bytes 69128 | tf_op jit(solution)/shard_map/ppermute | solution.py:24
  254.6 1.3 collective-permute-start.1
  256.0 28.9 %all-gather.17.cloned.1.call-done = bf16[768,1536]{1,0:T(8,128)(2,1)} async-done(((bf16[768,768]{1,0:T(8,128)(2,1)}), bf16[768,1536]{1,0:T(8,128)(2,1)}) %all-gather.17.cloned.1.call-update) | async-done | bytes 2359312 | tf_op jit(solution)/shard_map/all_gather | solution.py:114
  284.8 5.5 %convolution_convert_fusion = bf16[192,1536]{1,0:T(8,128)(2,1)} fusion(bf16[768,1536]{1,0:T(8,128)(2,1)} %all-gather.17.cloned.1.call-done, bf16[192,768]{1,0:T(8,128)(2,1)S(1)} %fusion.36, bf16[15,768]{1,0:T(8,128)(2,1)S(1)} %collective-permute-done.1, bf16[15,768]{1,0:T(8,128)(2,1)S(1)} %collective-permute-done, f32[768]{0:T(1024)S(1)} %get-tuple-element.34, ...), kind=kOutput, calls=%fused_computation | convolution fusion | flops 480854016 | bytes 3385344 | tf_op jit(solution)/shard_map/dot_general | solution.py:113
  290.3 8.1 %reduce-scatter.2.cloned.1.call-done = bf16[192,768]{1,0:T(8,128)(2,1)} async-done(((bf16[192,1536]{1,0:T(8,128)(2,1)}), bf16[192,768]{1,0:T(8,128)(2,1)}) %reduce-scatter.2.cloned.1.call-update) | async-done | bytes 294928 | tf_op jit(solution)/shard_map/reduce_scatter | solution.py:116
  298.5 1.7 fusion.37
  (40 shorter events, 6.1 us)
Async XLA Ops:
  7.4 46.9 %all-gather.9.cloned.1.call-start = ((), (), s32[]{:S(2)}) async-start(), calls=%async_computation.2 | async-start | bytes 1327104 | tf_op jit(solution)/shard_map/all_gather | solution.py:50
  8.1 88.7 %all-gather.11.cloned.1.call-start = ((), (), s32[]{:S(2)}) async-start(), calls=%async_computation.3 | async-start | bytes 1327104 | tf_op jit(solution)/shard_map/all_gather | solution.py:49
  8.8 130.0 %all-gather.7.cloned.1.call-start = ((), (), s32[]{:S(2)}) async-start(), calls=%async_computation.1 | async-start | bytes 1327104 | tf_op jit(solution)/shard_map/all_gather | solution.py:51
  9.6 171.8 %all-gather.13.cloned.1.call-start = ((), (), s32[]{:S(2)}) async-start(), calls=%async_computation.4 | async-start | bytes 1327104 | tf_op jit(solution)/shard_map/all_gather | solution.py:86
  10.1 191.6 %all-reduce.2.cloned.1.call-start = ((), (), s32[]{:S(2)}) async-start(), calls=%async_computation.5 | async-start | bytes 1179648 | tf_op jit(solution)/shard_map/psum | solution.py:89
  181.4 2.9 copy-start
  184.2 63.2 %all-gather.15.cloned.1.call-start = ((), (), s32[]{:S(2)}) async-start(), calls=%async_computation.6 | async-start | bytes 7077888 | tf_op jit(solution)/shard_map/all_gather | solution.py:98
  186.1 0.8 copy-start.1
  186.1 98.7 %all-gather.17.cloned.1.call-start = ((), (), s32[]{:S(2)}) async-start(), calls=%async_computation.7 | async-start | bytes 3538944 | tf_op jit(solution)/shard_map/all_gather | solution.py:114
  186.7 111.8 %reduce-scatter.2.cloned.1.call-start = ((), (), s32[]{:S(2)}) async-start(), calls=%async_computation.8 | async-start | bytes 884736 | tf_op jit(solution)/shard_map/reduce_scatter | solution.py:116
  251.2 33.7 %collective-permute-start = (bf16[15,768]{1,0:T(8,128)(2,1)S(1)}, bf16[15,768]{1,0:T(8,128)(2,1)S(1)}, u32[]{:S(2)}, u32[]{:S(2)}) collective-permute-start(bf16[15,768]{1,0:T(8,128)(2,1)S(1)} %get-tuple-element.38), channel_id=1, source_target_pairs={{0,4},{4,8},{8,12},{1,5},{5,9},{9,13},{2,6},{6,10},{10,14},{3,7},{... | collective-permute-start | bytes 69128 | tf_op jit(solution)/shard_map/ppermute | solution.py:24
  254.6 30.3 %collective-permute-start.1 = (bf16[15,768]{1,0:T(8,128)(2,1)S(1)}, bf16[15,768]{1,0:T(8,128)(2,1)S(1)}, u32[]{:S(2)}, u32[]{:S(2)}) collective-permute-start(bf16[15,768]{1,0:T(8,128)(2,1)S(1)} %get-tuple-element.39), channel_id=1, source_target_pairs={{4,0},{8,4},{12,8},{5,1},{9,5},{13,9},{6,2},{10,6},{14,10},{7,3},{... | collective-permute-start | bytes 69128 | tf_op jit(solution)/shard_map/ppermute | solution.py:26
Sparse Core Ops, SparseCore 0:
  10.3 43.8 all-gather.8
  56.4 40.3 all-gather.10
  99.0 39.8 all-gather.6
  140.9 40.4 all-gather.12
  184.4 17.3 all-reduce.1
  290.5 7.9 reduce-scatter.1
Sparse Core Ops, SparseCore 1:
  186.3 61.2 all-gather.14
  248.9 35.9 all-gather.16
where the time goes:
time: 308 us
  waiting for transfers between devices  222 us (72%)
  blocking collectives  38.7 us (13%)
  matrix products  18.5 us (6%)
  between operations  15.7 us (5%)
  other arithmetic  5.05 us (2%)
  starting transfers between devices  4.97 us (2%)
    all_gather x1, waiting for transfers between devices, shards(): lax.all_gather(w_glu, 'fsdp', axis=0, tiled=True)  44.1 us
    all_gather x1, waiting for transfers between devices, shards(): lax.all_gather(w_key, ('frames', 'fsdp'), axis=0, tiled=True)  40.3 us
    all_gather x1, waiting for transfers between devices, shards(): lax.all_gather(w_value, ('frames', 'fsdp'), axis=0, tiled=True)  40.1 us
    all_gather x1, waiting for transfers between devices, shards(): lax.all_gather(w_pw, 'fsdp', axis=1, tiled=True)  28.9 us
    all_gather x1, waiting for transfers between devices, shards(): lax.all_gather(w_query, ('frames', 'fsdp'), axis=0, tiled=True)  22.4 us
    all_gather x1, waiting for transfers between devices, shards(): lax.all_gather(w_out, ('frames', 'fsdp'), axis=1, tiled=True)  20.3 us
    all_gather x1, blocking collectives, shards(): lax.all_gather(key_rows, 'frames', axis=0, tiled=True)  18.1 us
    all_gather x1, blocking collectives, shards(): lax.all_gather(value_rows, 'frames', axis=0, tiled=True)  18.1 us
  transfers between devices with their start and end apart: 10, of which 8 were waited for; matrix products, arithmetic and copies ran while one was open for 5% of the time, Pallas kernels for 0%

commit v1 on v0

--- a/solution.py
+++ b/solution.py
@@ -1,9 +1,13 @@
+import functools
 import math
 
 import jax
 import jax.numpy as jnp
 from jax import lax
+from jax.experimental import pallas as pl
+from jax.experimental.pallas import tpu as pltpu
 from jax.sharding import PartitionSpec as P
+
 
 HEAD_DIM = 96
 KERNEL = 31
@@ -38,7 +42,11 @@
     return centred * lax.rsqrt(variance + EPS)
 
 
-def shards(frames_in, lengths, w_query, w_key, w_value, w_out, w_glu, dw_kernel, w_pw):
+def dot(a, b):
+    return jnp.dot(a, b, preferred_element_type=jnp.float32)
+
+
+def general_shards(frames_in, lengths, w_query, w_key, w_value, w_out, w_glu, dw_kernel, w_pw):
     full_rows = lax.all_gather(frames_in, "heads", axis=2, tiled=True)[0]
     frame_count = full_rows.shape[0]
     half_width = frames_in.shape[2]
@@ -50,17 +58,13 @@
         lax.all_gather(w_key, ("frames", "fsdp"), axis=0, tiled=True),
         lax.all_gather(w_value, ("frames", "fsdp"), axis=0, tiled=True),
     )
-    sliced = normed
-    projected = tuple(
-        (jnp.dot(sliced, piece_part, preferred_element_type=jnp.float32) for piece_part in pieces)
-    )
+    projected = tuple((dot(normed, piece_part) for piece_part in pieces))
     head_count = att_cols // HEAD_DIM
     queries = projected[0].astype(jnp.bfloat16).reshape(frame_count, head_count, HEAD_DIM)
     key_rows = projected[1].astype(jnp.bfloat16)
     value_rows = projected[2].astype(jnp.bfloat16)
     length = lengths[0]
     scale_factor = 1.0 / math.sqrt(HEAD_DIM)
-    start_max = jnp.full((frame_count, head_count), NEG_FILL, jnp.float32)
     pieces = (
         lax.all_gather(key_rows, "frames", axis=0, tiled=True),
         lax.all_gather(value_rows, "frames", axis=0, tiled=True),
@@ -74,27 +78,22 @@
     )
     valid = jnp.arange(block_rows, dtype=jnp.int32) < length
     masked = jnp.where(valid, scores, NEG_FILL)
-    new_max = jnp.maximum(start_max, jnp.max(masked, axis=2))
+    new_max = jnp.max(masked, axis=2)
     expo = jnp.where(valid, jnp.exp(masked - new_max[:, :, None]), 0.0)
     new_sum = jnp.sum(expo, axis=2)
     block_acc = jnp.einsum(
         "qhk,khd->qhd", expo.astype(jnp.bfloat16), value_block, preferred_element_type=jnp.float32
     )
     context = (block_acc / new_sum[:, :, None]).reshape(frame_count, att_cols).astype(jnp.bfloat16)
-    partial_value = jnp.dot(
-        context,
-        lax.all_gather(w_out, ("frames", "fsdp"), axis=1, tiled=True),
-        preferred_element_type=jnp.float32,
-    )
+    partial_value = dot(context, lax.all_gather(w_out, ("frames", "fsdp"), axis=1, tiled=True))
     total = lax.psum(partial_value.astype(jnp.bfloat16), "heads").astype(jnp.float32)
     stream_full = (full_rows.astype(jnp.float32) + total).astype(jnp.bfloat16)
     stream_own = lax.dynamic_slice_in_dim(stream_full, own_start, half_width, 1)
     normed_two = layer_norm(stream_full).astype(jnp.bfloat16)
     channels = w_glu.shape[2]
-    sliced = normed_two
     glu_pre = jnp.einsum(
         "td,dgc->tgc",
-        sliced,
+        normed_two,
         lax.all_gather(w_glu, "fsdp", axis=0, tiled=True),
         preferred_element_type=jnp.float32,
     )
@@ -110,14 +109,348 @@
             tap_index
         ].astype(jnp.float32)
     hidden = (depth * jax.nn.sigmoid(depth)).astype(jnp.bfloat16)
-    conv_part = jnp.dot(
-        hidden, lax.all_gather(w_pw, "fsdp", axis=1, tiled=True), preferred_element_type=jnp.float32
-    )
+    conv_part = dot(hidden, lax.all_gather(w_pw, "fsdp", axis=1, tiled=True))
     conv_half = lax.psum_scatter(
         conv_part.astype(jnp.bfloat16), "heads", scatter_dimension=1, tiled=True
     ).astype(jnp.float32)
     result = (stream_own.astype(jnp.float32) + conv_half).astype(jnp.bfloat16)
     return result[None]
+
+
+def swap(cells, axis, distance=1):
+    return lax.ppermute(cells, axis, [(i, i ^ distance) for i in range(lax.axis_size(axis))])
+
+
+def local(kernel, out_shape, args, scratch=(), flops=0, in_place=()):
+    out_bytes = sum(math.prod(s.shape) * s.dtype.itemsize for s in jax.tree.leaves(out_shape))
+    in_bytes = sum(math.prod(a.shape) * a.dtype.itemsize for a in args)
+    vmem = pl.BlockSpec(memory_space=pltpu.VMEM)
+    in_specs = [
+        pl.BlockSpec(memory_space=pltpu.SMEM)
+        if i == 0
+        else pl.BlockSpec(memory_space=pl.ANY)
+        if i in in_place
+        else vmem
+        for i in range(len(args))
+    ]
+    return pl.pallas_call(
+        kernel,
+        out_shape=out_shape,
+        in_specs=in_specs,
+        out_specs=jax.tree.map(lambda _: vmem, out_shape),
+        scratch_shapes=list(scratch),
+        cost_estimate=pl.CostEstimate(
+            flops=flops, bytes_accessed=in_bytes + out_bytes, transcendentals=0
+        ),
+    )(*args)
+
+
+def pack_kernel(pos, w_query, w_key, w_value, *outs):
+    count = len(outs)
+    groups = outs[0].shape[1] // (3 * HEAD_DIM)
+    size = outs[0].shape[0]
+    for here in range(count):
+
+        @pl.when(pos[0] == here)
+        def _():
+            for k, out in enumerate(outs):
+                first = (here ^ k) * HEAD_DIM
+                for part, w in enumerate((w_query, w_key, w_value)):
+                    for g in range(groups):
+                        at = (3 * g + part) * HEAD_DIM
+                        out[:, at : at + HEAD_DIM] = w[
+                            g * size : (g + 1) * size, first : first + HEAD_DIM
+                        ]
+
+
+def normalised(parts):
+    values = [p.astype(jnp.float32) for p in parts]
+    width = sum(v.shape[1] for v in values)
+    mean_row = sum(jnp.sum(v, axis=1, keepdims=True) for v in values) / width
+    centred = [v - mean_row for v in values]
+    variance = sum(jnp.sum(v * v, axis=1, keepdims=True) for v in centred) / width
+    scale = lax.rsqrt(variance + EPS)
+    return [(v * scale).astype(jnp.bfloat16) for v in centred]
+
+
+def projected(pos, own, other, weights):
+    half = own.shape[1]
+    total = 0.0
+    for flip, rows in enumerate(normalised((own[...], other[...]))):
+        at = pl.multiple_of((pos[3] ^ flip) * half, 128)
+        total = total + dot(rows, weights[pl.ds(at, half), :])
+    return total.astype(jnp.bfloat16)
+
+
+def early_kernel(count, pos, *refs):
+    packs, refs = refs[: 2 * count], refs[2 * count :]
+    outs, refs = refs[-3:], refs[:-3]
+    weights, three, window = outs
+    size, lanes = packs[0].shape
+    groups = lanes // weights.shape[1]
+    for k in range(count):
+        for other in range(2):
+            shard = 2 * (pos[0] ^ k) + (pos[1] ^ other)
+            for g in range(groups):
+                rows = pl.ds(pl.multiple_of(shard * (groups * size) + g * size, 16), size)
+                cols = slice(g * weights.shape[1], (g + 1) * weights.shape[1])
+                weights[rows, :] = packs[other * count + k][:, cols]
+    blocks = list(zip(refs[::2], refs[1::2]))
+    for i, (own, other) in enumerate(blocks):
+        three[i] = projected(pos, own, other, weights)
+    rows, half = blocks[0][0].shape
+    rim = (window.shape[0] - rows) // 2
+    odd = pos[0] % 2 == 1
+    for flip in range(2):
+        cols = pl.ds(pl.multiple_of((pos[3] ^ flip) * half, 128), half)
+        mine, near, far = (pair[flip] for pair in blocks)
+        window[rim : rim + rows, cols] = mine[...]
+        window[:rim, cols] = jnp.where(odd, near[rows - rim :, :], far[rows - rim :, :])
+        window[rim + rows :, cols] = jnp.where(odd, far[:rim, :], near[:rim, :])
+
+
+def attend_kernel(pos, own, other, weights, three, *refs):
+    outs, (joined, context) = refs[:-2], refs[-2:]
+    count = len(outs)
+    rows = own.shape[0]
+    rim = (outs[0].shape[0] - rows) // 2
+    for k, i in ((0, 0), (1, 1), (3, 2)):
+        joined[pl.ds(pl.multiple_of((pos[0] ^ k) * rows, 16), rows), :] = three[i]
+    at = pl.multiple_of((pos[0] ^ 2) * rows, 16)
+    joined[pl.ds(at, rows), :] = projected(pos, own, other, weights)
+    keys = joined[:, HEAD_DIM : 2 * HEAD_DIM]
+    values = joined[:, 2 * HEAD_DIM :]
+    valid = lax.broadcasted_iota(jnp.int32, (rows, count * rows), 1) < pos[4]
+    context[:rim, :] = jnp.zeros((rim, HEAD_DIM), jnp.bfloat16)
+    context[rim + count * rows :, :] = jnp.zeros((rim, HEAD_DIM), jnp.bfloat16)
+    for b in range(count):
+        scores = lax.dot_general(
+            joined[b * rows : (b + 1) * rows, :HEAD_DIM],
+            keys,
+            (((1,), (1,)), ((), ())),
+            preferred_element_type=jnp.float32,
+        ) * (1.0 / math.sqrt(HEAD_DIM))
+        masked = jnp.where(valid, scores, NEG_FILL)
+        row_max = jnp.max(masked, axis=1, keepdims=True)
+        expo = jnp.where(valid, jnp.exp(masked - row_max), 0.0)
+        denom = jnp.sum(expo, axis=1, keepdims=True)
+        mixed = dot(expo.astype(jnp.bfloat16), values) / denom
+        context[rim + b * rows : rim + (b + 1) * rows, :] = mixed.astype(jnp.bfloat16)
+    for k, out in enumerate(outs):
+        at = pl.multiple_of((pos[0] ^ k) * rows, 16)
+        out[...] = context[pl.ds(at, rows + 2 * rim), :]
+
+
+def out_kernel(pos, *refs):
+    count = (len(refs) - 3) // 3
+    pieces, first, second = refs[:count], refs[count : 2 * count], refs[2 * count : 3 * count]
+    out, by_head, weights = refs[-3:]
+    for k, piece in enumerate(pieces):
+        by_head[pos[0] ^ k] = piece[...]
+    joined = jnp.concatenate([by_head[h] for h in range(count)], axis=1)
+    cols = first[0].shape[0]
+    for k in range(count):
+        for flip, shard in ((0, first[k]), (1, second[k])):
+            at = pl.multiple_of((pos[2] ^ flip) * cols, 16)
+            weights[k, pl.ds(at, cols), :] = shard[...]
+        total = lax.dot_general(
+            joined, weights[k], (((1,), (1,)), ((), ())), preferred_element_type=jnp.float32
+        )
+        at = pl.multiple_of((pos[0] ^ k) * 2 * cols, 128)
+        out[:, pl.ds(at, 2 * cols)] = total.astype(jnp.bfloat16)
+
+
+def ffn_kernel(parts, pos, mine, theirs, window, taps, glu_own, *refs):
+    pieces, w_pw, refs = refs[: 2 * parts], refs[2 * parts], refs[2 * parts + 1 :]
+    stream_own, hidden_out, part_out, stream, normed, gated, w_a, w_b, w_c, w_d, sems = refs
+    copies = [pltpu.make_async_copy(glu_own, w_a, sems.at[0])]
+    for i, piece in enumerate(pieces):
+        target, at = (w_b, w_c)[i // parts], (i % parts) * piece.shape[1]
+        copies.append(
+            pltpu.make_async_copy(
+                piece, target.at[:, pl.ds(at, piece.shape[1]), :], sems.at[1 + i]
+            )
+        )
+    copies.append(pltpu.make_async_copy(w_pw, w_d, sems.at[1 + len(pieces)]))
+    for copy in copies:
+        copy.start()
+    wide, _ = window.shape
+    rows, half = stream_own.shape
+    rim = (wide - rows) // 2
+    total = mine[...].astype(jnp.float32) + theirs[...].astype(jnp.float32)
+    stream[...] = (window[...].astype(jnp.float32) + total).astype(jnp.bfloat16)
+    normed[...] = normalised((stream[...],))[0]
+    stream_own[...] = stream[
+        rim : rim + rows, pl.ds(pl.multiple_of(pos[3] * half, 128), half)
+    ]
+    quarter = half // 2
+    start = pl.multiple_of(pos[1] * half, 128)
+    lhs = [normed[:, pl.ds(start, half)]]
+    for flip in range(2):
+        start = pl.multiple_of((1 - pos[1]) * half + (pos[2] ^ flip) * quarter, 128)
+        lhs.append(normed[:, pl.ds(start, quarter)])
+    pre = [0.0, 0.0]
+    for j, (cols, w) in enumerate(zip(lhs, (w_a, w_b, w_c))):
+        for copy in copies[:1] if j == 0 else copies[1 + (j - 1) * parts : 1 + j * parts]:
+            copy.wait()
+        pre = [pre[g] + dot(cols, w[g]) for g in range(2)]
+    positions = pos[0] * rows - rim + lax.broadcasted_iota(jnp.int32, (wide, 1), 0)
+    live = (positions >= 0) & (positions < pos[4])
+    product = jnp.where(live, pre[0] * jax.nn.sigmoid(pre[1]), 0.0)
+    gated[...] = product.astype(jnp.bfloat16).astype(jnp.float32)
+    first = rim - KERNEL // 2
+    for lane in range(0, half, 128):
+        depth = jnp.zeros((rows, 128), jnp.float32)
+        for tap in range(KERNEL):
+            depth = depth + gated[first + tap : first + tap + rows, lane : lane + 128] * taps[
+                tap : tap + 1, lane : lane + 128
+            ].astype(jnp.float32)
+        hidden_out[:, lane : lane + 128] = (depth * jax.nn.sigmoid(depth)).astype(jnp.bfloat16)
+    copies[-1].wait()
+    part_out[...] = dot(hidden_out[...], w_d[...]).astype(jnp.bfloat16)
+
+
+def pw_kernel(parts, pos, hidden, part_own, *refs):
+    pieces, (keep, send) = refs[: 2 * parts], refs[2 * parts :]
+    quarter = hidden.shape[1] // 2
+    total = 0.0
+    for flip in range(2):
+        at = pl.multiple_of((pos[2] ^ flip) * quarter, 128)
+        cols = hidden[:, pl.ds(at, quarter)]
+        size = quarter // parts
+        for i in range(parts):
+            total = total + dot(cols[:, i * size : (i + 1) * size], pieces[flip * parts + i][...])
+    other = total.astype(jnp.bfloat16)
+    same = pos[1] == pos[3]
+    keep[...] = jnp.where(same, part_own[...], other)
+    send[...] = jnp.where(same, other, part_own[...])
+
+
+def head_shards(frames_in, lengths, w_query, w_key, w_value, w_out, w_glu, dw_kernel, w_pw):
+    bf16 = jnp.bfloat16
+    blocks = lax.axis_size("frames")
+    z = lax.axis_index("frames")
+    x = lax.axis_index("fsdp")
+    y = lax.axis_index("groups")
+    c = lax.axis_index("heads")
+    own = frames_in[0]
+    rows, half = own.shape
+    length = lengths[0]
+    rim = 16 * (-(-(KERNEL // 2) // 16))
+    wide = rows + 2 * rim
+    pos = jnp.stack([z, x, y, c, length]).astype(jnp.int32)
+
+    def shape(*dims):
+        return jax.ShapeDtypeStruct(dims, bf16)
+
+    far = swap(own, "frames", 3)
+    c_own = swap(own, "heads", 1)
+    near = swap(own, "frames", 1)
+    relayed = swap(far, "frames", 1)
+    c_near = swap(near, "heads", 1)
+    c_far = swap(far, "heads", 1)
+    c_relayed = swap(relayed, "heads", 1)
+
+    groups = 128 // math.gcd(128, 3 * HEAD_DIM)
+    packed = local(
+        pack_kernel,
+        [shape(w_query.shape[0] // groups, groups * 3 * HEAD_DIM)] * blocks,
+        (pos, w_query, w_key, w_value),
+    )
+    w_mine = [packed[0]] + [swap(packed[k], "frames", k) for k in range(1, blocks)]
+    w_other = [swap(w_mine[k], "fsdp", 1) for k in range(blocks)]
+
+    out_own = w_out.T
+    out_other = swap(out_own, "fsdp", 1)
+    out_send = jnp.where(x == y, out_own, out_other)
+    out_keep = jnp.where(x == y, out_other, out_own)
+    out_far = swap(out_send, "frames", 3)
+    out_near = swap(out_send, "frames", 1)
+    out_relayed = swap(out_far, "frames", 1)
+    out_first = [out_send, out_near, out_relayed, out_far]
+    out_second = [out_keep] + [swap(out_first[k], "groups", 1) for k in range(1, blocks)]
+
+    glu_own = w_glu.transpose(1, 0, 2)
+    glu_rows = glu_own.shape[1] // 2
+    chunk = glu_rows // GLU_PARTS
+    glu_a = [
+        swap(lax.dynamic_slice_in_dim(glu_own, y * glu_rows + i * chunk, chunk, 1), "fsdp", 1)
+        for i in range(GLU_PARTS)
+    ]
+    glu_b = [swap(t, "groups", 1) for t in glu_a]
+    pw_rows = w_pw.shape[0] // 2
+    chunk_pw = pw_rows // PW_PARTS
+    pw_a = [
+        swap(lax.dynamic_slice_in_dim(w_pw, y * pw_rows + i * chunk_pw, chunk_pw, 0), "fsdp", 1)
+        for i in range(PW_PARTS)
+    ]
+    pw_b = [swap(t, "groups", 1) for t in pw_a]
+
+    w_full, three, window = local(
+        functools.partial(early_kernel, blocks),
+        [
+            shape(2 * blocks * rows, 3 * HEAD_DIM),
+            shape(3, rows, 3 * HEAD_DIM),
+            shape(wide, 2 * half),
+        ],
+        (pos, *w_mine, *w_other, own, c_own, near, c_near, far, c_far),
+        flops=6 * rows * 2 * half * 3 * HEAD_DIM,
+    )
+    windows = local(
+        attend_kernel,
+        [shape(wide, HEAD_DIM)] * blocks,
+        (pos, relayed, c_relayed, w_full, three),
+        [
+            pltpu.VMEM((blocks * rows, 3 * HEAD_DIM), bf16),
+            pltpu.VMEM((blocks * rows + 2 * rim, HEAD_DIM), bf16),
+        ],
+        flops=4 * (blocks * rows) ** 2 * HEAD_DIM,
+    )
+
+    heads_in = [windows[0]] + [swap(windows[k], "frames", k) for k in range(1, blocks)]
+    partial_value = local(
+        out_kernel,
+        shape(wide, 2 * half),
+        (pos, *heads_in, *out_first, *out_second),
+        [
+            pltpu.VMEM((blocks, wide, HEAD_DIM), bf16),
+            pltpu.VMEM((blocks, 2 * out_own.shape[0], out_own.shape[1]), bf16),
+        ],
+        flops=2 * wide * blocks * HEAD_DIM * 2 * half,
+    )
+    partial_other = swap(partial_value, "heads", 1)
+
+    channels = w_glu.shape[2]
+    stream_own, hidden, part_own = local(
+        functools.partial(ffn_kernel, GLU_PARTS),
+        [shape(rows, half), shape(rows, channels), shape(rows, w_pw.shape[1])],
+        (pos, partial_value, partial_other, window, dw_kernel, glu_own, *glu_a, *glu_b, w_pw),
+        [
+            pltpu.VMEM((wide, 2 * half), bf16),
+            pltpu.VMEM((wide, 2 * half), bf16),
+            pltpu.VMEM((wide, channels), jnp.float32),
+            pltpu.VMEM(glu_own.shape, bf16),
+            pltpu.VMEM((2, glu_rows, channels), bf16),
+            pltpu.VMEM((2, glu_rows, channels), bf16),
+            pltpu.VMEM(w_pw.shape, bf16),
+            pltpu.SemaphoreType.DMA((2 + 2 * GLU_PARTS,)),
+        ],
+        flops=8 * wide * half * channels,
+        in_place=range(5, 7 + 2 * GLU_PARTS),
+    )
+    keep, send = local(
+        functools.partial(pw_kernel, PW_PARTS),
+        [shape(rows, w_pw.shape[1])] * 2,
+        (pos, hidden, part_own, *pw_a, *pw_b),
+        flops=2 * rows * channels * half,
+    )
+    arrived = swap(send, "heads", 1)
+    conv = keep.astype(jnp.float32) + arrived.astype(jnp.float32)
+    return (stream_own.astype(jnp.float32) + conv).astype(bf16)[None]
+
+
+GLU_PARTS = 2
+PW_PARTS = 1
 
 
 def solution(mesh):
@@ -133,4 +466,12 @@
         P("heads", "fsdp"),
     )
     out_specs = P(("groups", "fsdp"), "frames", "heads")
+    sizes = mesh.shape
+    by_mesh = sizes["frames"] == 4 and sizes["fsdp"] == sizes["groups"] == sizes["heads"] == 2
+
+    def shards(*args):
+        if not (by_mesh and args[2].shape[1] == sizes["frames"] * HEAD_DIM):
+            return general_shards(*args)
+        return head_shards(*args)
+
     return jax.shard_map(shards, mesh=mesh, in_specs=in_specs, out_specs=out_specs, check_vma=False)

time: 308 us -> 128 us (0.42)
  waiting for transfers between devices: 222 us -> 51 us
  blocking collectives: 38.7 us -> 0 us
  starting transfers between devices: 4.97 us -> 37.8 us
  Pallas kernels: 0 us -> 26.5 us
  matrix products: 18.5 us -> 0 us
  between operations: 15.7 us -> 0.78 us
  local copies, waits for them, and re-layouts: 2.57 us -> 7.74 us
    all_gather x6 -> x0, waiting for transfers between devices: 196 us -> none  [the longest x1 44.1 us: shards(): lax.all_gather(w_glu, 'fsdp', axis=0, tiled=True)]
    ppermute x2 -> x32, waiting for transfers between devices: 0.01 us -> 51 us  [swap(): lax.ppermute(cells, axis, [(i, i ^ distance) for i in range(lax.axis_size...]
    all_gather x3 -> x0, blocking collectives: 38.7 us -> none  [the longest x1 18.1 us: shards(): lax.all_gather(key_rows, 'frames', axis=0, tiled=True)]
    ppermute x2 -> x32, starting transfers between devices: 4.68 us -> 37.8 us  [swap(): lax.ppermute(cells, axis, [(i, i ^ distance) for i in range(lax.axis_size...]
    pallas_call x0 -> x6, Pallas kernels: none -> 26.5 us  [local(): pl.pallas_call(kernel, out_shape=out_shape, in_specs=in_specs, out_specs=...]
    dot_general x8 -> x0, matrix products: 18.5 us -> none  [the longest x1 5.47 us: shards(): jnp.dot(hidden, lax.all_gather(w_pw, 'fsdp', axis=1, tiled=True), preferr...]
    psum x1 -> x0, waiting for transfers between devices: 14.7 us -> none  [shards(): lax.psum(partial_value.astype(jnp.bfloat16), 'heads').astype(jnp.float32)]
    reduce_scatter x1 -> x0, waiting for transfers between devices: 8.11 us -> none  [shards(): lax.psum_scatter(conv_part.astype(jnp.bfloat16), 'heads', scatter_dimensi...]
  transfers between devices with their start and end apart: 10 -> 32, of which waited for: 8 -> 12; matrix products, arithmetic and copies ran while one was open for 5% -> 4% of each run, Pallas kernels for 0% -> 17%
where the time goes in v1:
time: 128 us; the launch traced here: 127 us
  waiting for transfers between devices  51 us (40%)
  starting transfers between devices  37.8 us (30%)
  Pallas kernels  26.5 us (21%)
  local copies, waits for them, and re-layouts  7.74 us (6%)
  other arithmetic  3.55 us (3%)
    ppermute x32, waiting for transfers between devices, swap(): lax.ppermute(cells, axis, [(i, i ^ distance) for i in range(lax.axis_size...  51 us
    ppermute x32, starting transfers between devices, swap(): lax.ppermute(cells, axis, [(i, i ^ distance) for i in range(lax.axis_size...  37.8 us
    pallas_call x6, Pallas kernels, local(): pl.pallas_call(kernel, out_shape=out_shape, in_specs=in_specs, out_specs=...  26.5 us
    unnamed x39, local copies, waits for them, and re-layouts  5.07 us
  transfers between devices with their start and end apart: 32, of which 12 were waited for; matrix products, arithmetic and copies ran while one was open for 4% of the time, Pallas kernels for 17%

profile of v1, /device:TPU:0, one launch (start us, length us, event | category | flops | bytes accessed | tf_op | source)
XLA Modules:
  0.0 127.3 jit_solution(11266703650414303707)
XLA Ops:
  1.3 2.1 %shard_map.91 = (bf16[48,1152]{1,0:T(8,128)(2,1)}, bf16[48,1152]{1,0:T(8,128)(2,1)}, bf16[48,1152]{1,0:T(8,128)(2,1)}, bf16[48,1152]{1,0:T(8,128)(2,1)}) custom-call(s32[5]{0:T(128)} %stack.19.pos, bf16[192,384]{1,0:T(8,128)(2,1)} %w_query.1, bf16[192,384]{1,0:T(8,128)(2,1)} %w_key.1, bf16[192,384]{1,0:T(8,128)(2,1)} %w_value.1), custom_call_target="tpu_custom_call" | custom-call | bytes 884756 | tf_op jit(solution)/shard_map/pallas_call | solution.py:136
  3.5 3.1 %collective-permute-start.3 = (bf16[48,1152]{1,0:T(8,128)(2,1)}, bf16[48,1152]{1,0:T(8,128)(2,1)S(1)}, u32[]{:S(2)}, u32[]{:S(2)}) collective-permute-start(bf16[48,1152]{1,0:T(8,128)(2,1)} %get-tuple-element.22), channel_id=1, source_target_pairs={{0,4},{4,0},{8,12},{12,8},{1,5},{5,1},{9,13},{13,9},{2,6},{6,2},{1... | collective-permute-start | bytes 331784 | tf_op jit(solution)/shard_map/ppermute | solution.py:121
  6.5 2.6 %collective-permute-start.4 = (bf16[48,1152]{1,0:T(8,128)(2,1)}, bf16[48,1152]{1,0:T(8,128)(2,1)S(1)}, u32[]{:S(2)}, u32[]{:S(2)}) collective-permute-start(bf16[48,1152]{1,0:T(8,128)(2,1)} %get-tuple-element.23), channel_id=1, source_target_pairs={{0,8},{4,12},{8,0},{12,4},{1,9},{5,13},{9,1},{13,5},{2,10},{6,14},... | collective-permute-start | bytes 331784 | tf_op jit(solution)/shard_map/ppermute | solution.py:121
  12.8 4.7 %collective-permute-done.4.refs_2_ = bf16[48,1152]{1,0:T(8,128)(2,1)S(1)} collective-permute-done((bf16[48,1152]{1,0:T(8,128)(2,1)}, bf16[48,1152]{1,0:T(8,128)(2,1)S(1)}, u32[]{:S(2)}, u32[]{:S(2)}) %collective-permute-start.4) | collective-permute-done | bytes 110624 | tf_op jit(solution)/shard_map/ppermute | solution.py:121
  17.6 3.0 %collective-permute-start = (bf16[192,768]{1,0:T(8,128)(2,1)}, bf16[192,768]{1,0:T(8,128)(2,1)}, u32[]{:S(2)}, u32[]{:S(2)}) collective-permute-start(bf16[192,768]{1,0:T(8,128)(2,1)} %bitcast.17), channel_id=1, source_target_pairs={{0,12},{4,8},{8,4},{12,0},{1,13},{5,9},{9,5},{13,1},{2,14},{6,10},... | collective-permute-start | bytes 884744 | tf_op jit(solution)/shard_map/ppermute | solution.py:121
  20.5 3.1 %collective-permute-start.11 = (bf16[192,768]{1,0:T(8,128)(2,1)}, bf16[192,768]{1,0:T(8,128)(2,1)}, u32[]{:S(2)}, u32[]{:S(2)}) collective-permute-start(bf16[192,768]{1,0:T(8,128)(2,1)} %bitcast.18), channel_id=1, source_target_pairs={{0,4},{4,0},{8,12},{12,8},{1,5},{5,1},{9,13},{13,9},{2,6},{6,2},{1... | collective-permute-start | bytes 884744 | tf_op jit(solution)/shard_map/ppermute | solution.py:121
  23.7 2.0 %collective-permute-start.8 = (bf16[48,1152]{1,0:T(8,128)(2,1)S(1)}, bf16[48,1152]{1,0:T(8,128)(2,1)S(1)}, u32[]{:S(2)}, u32[]{:S(2)}) collective-permute-start(bf16[48,1152]{1,0:T(8,128)(2,1)S(1)} %collective-permute-done.4.refs_2_), channel_id=1, source_target_pairs={{0,2},{2,0},{1,3},{3,1},{4,6},{6,4},{5,7},{7,5},{8,10},{10,8},{9,1... | collective-permute-start | bytes 331784 | tf_op jit(solution)/shard_map/ppermute | solution.py:121
  27.5 2.2 %collective-permute-done.8.refs_6_ = bf16[48,1152]{1,0:T(8,128)(2,1)S(1)} collective-permute-done((bf16[48,1152]{1,0:T(8,128)(2,1)S(1)}, bf16[48,1152]{1,0:T(8,128)(2,1)S(1)}, u32[]{:S(2)}, u32[]{:S(2)}) %collective-permute-start.8) | collective-permute-done | bytes 110624 | tf_op jit(solution)/shard_map/ppermute | solution.py:121
  30.2 3.2 %collective-permute-start.1 = (bf16[192,768]{1,0:T(8,128)(2,1)}, bf16[192,768]{1,0:T(8,128)(2,1)}, u32[]{:S(2)}, u32[]{:S(2)}) collective-permute-start(bf16[192,768]{1,0:T(8,128)(2,1)} %collective-permute-done.refs_12_), channel_id=1, source_target_pairs={{0,4},{4,0},{8,12},{12,8},{1,5},{5,1},{9,13},{13,9},{2,6},{6,2},{1... | collective-permute-start | bytes 884744 | tf_op jit(solution)/shard_map/ppermute | solution.py:121
  34.0 4.5 %collective-permute-done.19.refs_7_ = bf16[192,384]{1,0:T(8,128)(2,1)} collective-permute-done((bf16[192,384]{1,0:T(8,128)(2,1)}, bf16[192,384]{1,0:T(8,128)(2,1)}, u32[]{:S(2)}, u32[]{:S(2)}) %collective-permute-start.19) | collective-permute-done | bytes 147488 | tf_op jit(solution)/shard_map/ppermute | solution.py:121
  40.3 2.0 %copy.15 = bf16[768,2,768]{2,0,1:T(8,128)(2,1)S(1)} copy(bf16[768,2,768]{2,1,0:T(2,128)(2,1)} %param.15) | data formatting | bytes 4718592 | tf_op args[6]
  42.3 4.4 %collective-permute-done.18.refs_5_ = bf16[192,384]{1,0:T(8,128)(2,1)} collective-permute-done((bf16[192,384]{1,0:T(8,128)(2,1)}, bf16[192,384]{1,0:T(8,128)(2,1)}, u32[]{:S(2)}, u32[]{:S(2)}) %collective-permute-start.18) | collective-permute-done | bytes 147488 | tf_op jit(solution)/shard_map/ppermute | solution.py:121
  55.0 4.8 %shard_map.92 = (bf16[1536,288]{1,0:T(8,128)(2,1)}, bf16[3,192,288]{2,1,0:T(8,128)(2,1)}, bf16[224,1536]{1,0:T(8,128)(2,1)}) custom-call(s32[5]{0:T(128)} %stack.19.pos, bf16[48,1152]{1,0:T(8,128)(2,1)} %get-tuple-element.21.refs_0_, bf16[48,1152]{1,0:T(8,128)(2,1)} %copy-done.9, bf16[48,1152]{1,0:T(8,128)(2,1)} %copy-done.10, bf16[48,1152]{1,0:T(8,128)(2,1)} %copy-done.11, ...), custom_call_target="tpu_custom_call" | custom-call | flops 509607936 | bytes 4558868 | tf_op jit(solution)/shard_map/pallas_call | solution.py:136
  59.8 4.8 %shard_map.93 = (bf16[224,96]{1,0:T(8,128)(2,1)}, bf16[224,96]{1,0:T(8,128)(2,1)}, bf16[224,96]{1,0:T(8,128)(2,1)}, bf16[224,96]{1,0:T(8,128)(2,1)}) custom-call(s32[5]{0:T(128)} %stack.19.pos, bf16[192,768]{1,0:T(8,128)(2,1)} %collective-permute-done.1.own, bf16[192,768]{1,0:T(8,128)(2,1)} %collective-permute-done.2.other, ...), custom_call_target="tpu_custom_call" | custom-call | flops 226492416 | bytes 1978388 | tf_op jit(solution)/shard_map/pallas_call | solution.py:136
  69.1 3.0 %collective-permute-start.16 = (bf16[224,96]{1,0:T(8,128)(2,1)}, bf16[224,96]{1,0:T(8,128)(2,1)S(1)}, u32[]{:S(2)}, u32[]{:S(2)}) collective-permute-start(bf16[224,96]{1,0:T(8,128)(2,1)} %get-tuple-element.30), channel_id=1, source_target_pairs={{0,12},{4,8},{8,4},{12,0},{1,13},{5,9},{9,5},{13,1},{2,14},{6,10},... | collective-permute-start | bytes 129032 | tf_op jit(solution)/shard_map/ppermute | solution.py:121
  72.1 3.2 %collective-permute-done.16.refs_3_ = bf16[224,96]{1,0:T(8,128)(2,1)S(1)} collective-permute-done((bf16[224,96]{1,0:T(8,128)(2,1)}, bf16[224,96]{1,0:T(8,128)(2,1)S(1)}, u32[]{:S(2)}, u32[]{:S(2)}) %collective-permute-start.16) | collective-permute-done | bytes 43040 | tf_op jit(solution)/shard_map/ppermute | solution.py:121
  75.9 3.0 %shard_map.94.mine = bf16[224,1536]{1,0:T(8,128)(2,1)} custom-call(s32[5]{0:T(128)} %stack.19.pos, bf16[224,96]{1,0:T(8,128)(2,1)} %get-tuple-element.27.refs_0_, bf16[224,96]{1,0:T(8,128)(2,1)} %copy-done.16, bf16[224,96]{1,0:T(8,128)(2,1)} %copy-done.17, bf16[224,96]{1,0:T(8,128)(2,1)} %copy-done.18, bf16[192,384]{1,0:T(8,128)(2,1)} %get-tuple-element.42.refs_4_, ...), custom_call_target="tpu_custom_call" | custom-call | flops 264241152 | bytes 2039828 | tf_op jit(solution)/shard_map/pallas_call | solution.py:136
  81.0 8.1 %collective-permute-done.29.refs_0_ = bf16[384,768]{1,0:T(8,128)(2,1)S(1)} collective-permute-done((bf16[384,768]{1,0:T(8,128)(2,1)}, bf16[384,768]{1,0:T(8,128)(2,1)S(1)}, u32[]{:S(2)}, u32[]{:S(2)}) %collective-permute-start.29) | collective-permute-done | bytes 589856 | tf_op jit(solution)/shard_map/ppermute | solution.py:121
  90.6 4.8 %collective-permute-done.27.refs_2_ = bf16[2,192,768]{2,1,0:T(8,128)(2,1)S(1)} collective-permute-done((bf16[2,192,768]{2,1,0:T(8,128)(2,1)}, bf16[2,192,768]{2,1,0:T(8,128)(2,1)S(1)}, u32[]{:S(2)}, u32[]{:S(2)}) %collective-permute-start.27) | collective-permute-done | bytes 589856 | tf_op jit(solution)/shard_map/ppermute | solution.py:121
  95.4 12.6 %collective-permute-done.28.refs_3_ = bf16[2,192,768]{2,1,0:T(8,128)(2,1)S(1)} collective-permute-done((bf16[2,192,768]{2,1,0:T(8,128)(2,1)}, bf16[2,192,768]{2,1,0:T(8,128)(2,1)S(1)}, u32[]{:S(2)}, u32[]{:S(2)}) %collective-permute-start.28) | collective-permute-done | bytes 589856 | tf_op jit(solution)/shard_map/ppermute | solution.py:121
  109.1 9.0 %shard_map.95 = (bf16[192,768]{1,0:T(8,128)(2,1)}, bf16[192,768]{1,0:T(8,128)(2,1)}, bf16[192,768]{1,0:T(8,128)(2,1)}) custom-call(s32[5]{0:T(128)} %stack.19.pos, bf16[224,1536]{1,0:T(8,128)(2,1)} %shard_map.94.mine, bf16[224,1536]{1,0:T(8,128)(2,1)} %copy-done.2, bf16[224,1536]{1,0:T(8,128)(2,1)} %get-tuple-element.31.window, bf16[31,768]{1,0:T(8,128)(2,1)} %taps.1, ...), custom_call_target="tpu_custom_call" | custom-call | flops 1056964608 | bytes 8894996 | tf_op jit(solution)/shard_map/pallas_call | solution.py:136
  118.1 2.0 %collective-permute-done.30.refs_1_ = bf16[384,768]{1,0:T(8,128)(2,1)S(1)} collective-permute-done((bf16[384,768]{1,0:T(8,128)(2,1)S(1)}, bf16[384,768]{1,0:T(8,128)(2,1)S(1)}, u32[]{:S(2)}, u32[]{:S(2)}) %collective-permute-start.30) | collective-permute-done | bytes 589856 | tf_op jit(solution)/shard_map/ppermute | solution.py:121
  121.0 2.7 %shard_map.96 = (bf16[192,768]{1,0:T(8,128)(2,1)}, bf16[192,768]{1,0:T(8,128)(2,1)}) custom-call(s32[5]{0:T(128)} %stack.19.pos, bf16[192,768]{1,0:T(8,128)(2,1)} %get-tuple-element.33.hidden, bf16[192,768]{1,0:T(8,128)(2,1)} %get-tuple-element.34.part_own, bf16[384,768]{1,0:T(8,128)(2,1)} %copy-done.5, bf16[384,768]{1,0:T(8,128)(2,1)} %copy-done.6), custom_call_target="tpu_custom_call" | custom-call | flops 226492416 | bytes 2359316 | tf_op jit(solution)/shard_map/pallas_call | solution.py:136
  125.5 1.9 %fusion = bf16[1,192,768]{2,1,0:T(8,128)(2,1)} fusion(bf16[192,768]{1,0:T(8,128)(2,1)S(1)} %collective-permute-done.31, bf16[192,768]{1,0:T(8,128)(2,1)} %get-tuple-element.35, bf16[192,768]{1,0:T(8,128)(2,1)} %get-tuple-element.32), kind=kLoop, calls=%fused_computation.3 | loop fusion | flops 884736 | bytes 1179648 | tf_op jit(solution)/shard_map/broadcast_in_dim | solution.py:449
  (90 shorter events, 29.8 us)
Async XLA Ops:
  3.5 7.7 %collective-permute-start.3 = (bf16[48,1152]{1,0:T(8,128)(2,1)}, bf16[48,1152]{1,0:T(8,128)(2,1)S(1)}, u32[]{:S(2)}, u32[]{:S(2)}) collective-permute-start(bf16[48,1152]{1,0:T(8,128)(2,1)} %get-tuple-element.22), channel_id=1, source_target_pairs={{0,4},{4,0},{8,12},{12,8},{1,5},{5,1},{9,13},{13,9},{2,6},{6,2},{1... | collective-permute-start | bytes 331784 | tf_op jit(solution)/shard_map/ppermute | solution.py:121
  6.5 11.1 %collective-permute-start.4 = (bf16[48,1152]{1,0:T(8,128)(2,1)}, bf16[48,1152]{1,0:T(8,128)(2,1)S(1)}, u32[]{:S(2)}, u32[]{:S(2)}) collective-permute-start(bf16[48,1152]{1,0:T(8,128)(2,1)} %get-tuple-element.23), channel_id=1, source_target_pairs={{0,8},{4,12},{8,0},{12,4},{1,9},{5,13},{9,1},{13,5},{2,10},{6,14},... | collective-permute-start | bytes 331784 | tf_op jit(solution)/shard_map/ppermute | solution.py:121
  9.1 14.6 %collective-permute-start.17 = (bf16[192,384]{1,0:T(8,128)(2,1)}, bf16[192,384]{1,0:T(8,128)(2,1)S(1)}, u32[]{:S(2)}, u32[]{:S(2)}) collective-permute-start(bf16[192,384]{1,0:T(8,128)(2,1)} %bitcast.21), channel_id=1, source_target_pairs={{0,2},{2,0},{1,3},{3,1},{4,6},{6,4},{5,7},{7,5},{8,10},{10,8},{9,1... | collective-permute-start | bytes 442376 | tf_op jit(solution)/shard_map/ppermute | solution.py:121
  10.6 9.9 %collective-permute-start.5 = (bf16[48,1152]{1,0:T(8,128)(2,1)}, bf16[48,1152]{1,0:T(8,128)(2,1)S(1)}, u32[]{:S(2)}, u32[]{:S(2)}) collective-permute-start(bf16[48,1152]{1,0:T(8,128)(2,1)} %get-tuple-element.24), channel_id=1, source_target_pairs={{0,12},{4,8},{8,4},{12,0},{1,13},{5,9},{9,5},{13,1},{2,14},{6,10},... | collective-permute-start | bytes 331784 | tf_op jit(solution)/shard_map/ppermute | solution.py:121
  10.8 12.9 %collective-permute-start.6 = (bf16[48,1152]{1,0:T(8,128)(2,1)}, bf16[48,1152]{1,0:T(8,128)(2,1)S(1)}, u32[]{:S(2)}, u32[]{:S(2)}) collective-permute-start(bf16[48,1152]{1,0:T(8,128)(2,1)} %get-tuple-element.21.refs_0_), channel_id=1, source_target_pairs={{0,2},{2,0},{1,3},{3,1},{4,6},{6,4},{5,7},{7,5},{8,10},{10,8},{9,1... | collective-permute-start | bytes 331784 | tf_op jit(solution)/shard_map/ppermute | solution.py:121
  11.1 14.6 %collective-permute-start.7 = (bf16[48,1152]{1,0:T(8,128)(2,1)S(1)}, bf16[48,1152]{1,0:T(8,128)(2,1)S(1)}, u32[]{:S(2)}, u32[]{:S(2)}) collective-permute-start(bf16[48,1152]{1,0:T(8,128)(2,1)S(1)} %collective-permute-done.3.refs_1_), channel_id=1, source_target_pairs={{0,2},{2,0},{1,3},{3,1},{4,6},{6,4},{5,7},{7,5},{8,10},{10,8},{9,1... | collective-permute-start | bytes 331784 | tf_op jit(solution)/shard_map/ppermute | solution.py:121
  17.6 12.6 %collective-permute-start = (bf16[192,768]{1,0:T(8,128)(2,1)}, bf16[192,768]{1,0:T(8,128)(2,1)}, u32[]{:S(2)}, u32[]{:S(2)}) collective-permute-start(bf16[192,768]{1,0:T(8,128)(2,1)} %bitcast.17), channel_id=1, source_target_pairs={{0,12},{4,8},{8,4},{12,0},{1,13},{5,9},{9,5},{13,1},{2,14},{6,10},... | collective-permute-start | bytes 884744 | tf_op jit(solution)/shard_map/ppermute | solution.py:121
  20.5 13.5 %collective-permute-start.11 = (bf16[192,768]{1,0:T(8,128)(2,1)}, bf16[192,768]{1,0:T(8,128)(2,1)}, u32[]{:S(2)}, u32[]{:S(2)}) collective-permute-start(bf16[192,768]{1,0:T(8,128)(2,1)} %bitcast.18), channel_id=1, source_target_pairs={{0,4},{4,0},{8,12},{12,8},{1,5},{5,1},{9,13},{13,9},{2,6},{6,2},{1... | collective-permute-start | bytes 884744 | tf_op jit(solution)/shard_map/ppermute | solution.py:121
  23.7 15.1 %collective-permute-start.10 = (bf16[192,768]{1,0:T(8,128)(2,1)}, bf16[192,768]{1,0:T(8,128)(2,1)}, u32[]{:S(2)}, u32[]{:S(2)}) collective-permute-start(bf16[192,768]{1,0:T(8,128)(2,1)} %bitcast.19), channel_id=1, source_target_pairs={{0,1},{1,0},{2,3},{3,2},{4,5},{5,4},{6,7},{7,6},{8,9},{9,8},{10,11... | collective-permute-start | bytes 884744 | tf_op jit(solution)/shard_map/ppermute | solution.py:121
  29.7 8.8 %collective-permute-start.19 = (bf16[192,384]{1,0:T(8,128)(2,1)}, bf16[192,384]{1,0:T(8,128)(2,1)}, u32[]{:S(2)}, u32[]{:S(2)}) collective-permute-start(bf16[192,384]{1,0:T(8,128)(2,1)} %get-tuple-element.42.refs_4_), channel_id=1, source_target_pairs={{0,12},{4,8},{8,4},{12,0},{1,13},{5,9},{9,5},{13,1},{2,14},{6,10},... | collective-permute-start | bytes 442376 | tf_op jit(solution)/shard_map/ppermute | solution.py:121
  30.2 20.9 %collective-permute-start.1 = (bf16[192,768]{1,0:T(8,128)(2,1)}, bf16[192,768]{1,0:T(8,128)(2,1)}, u32[]{:S(2)}, u32[]{:S(2)}) collective-permute-start(bf16[192,768]{1,0:T(8,128)(2,1)} %collective-permute-done.refs_12_), channel_id=1, source_target_pairs={{0,4},{4,0},{8,12},{12,8},{1,5},{5,1},{9,13},{13,9},{2,6},{6,2},{1... | collective-permute-start | bytes 884744 | tf_op jit(solution)/shard_map/ppermute | solution.py:121
  33.4 13.4 %collective-permute-start.18 = (bf16[192,384]{1,0:T(8,128)(2,1)}, bf16[192,384]{1,0:T(8,128)(2,1)}, u32[]{:S(2)}, u32[]{:S(2)}) collective-permute-start(bf16[192,384]{1,0:T(8,128)(2,1)} %get-tuple-element.42.refs_4_), channel_id=1, source_target_pairs={{0,4},{4,0},{8,12},{12,8},{1,5},{5,1},{9,13},{13,9},{2,6},{6,2},{1... | collective-permute-start | bytes 442376 | tf_op jit(solution)/shard_map/ppermute | solution.py:121
  34.0 18.0 %collective-permute-start.13 = (bf16[192,768]{1,0:T(8,128)(2,1)}, bf16[192,768]{1,0:T(8,128)(2,1)}, u32[]{:S(2)}, u32[]{:S(2)}) collective-permute-start(bf16[192,768]{1,0:T(8,128)(2,1)} %collective-permute-done.refs_12_), channel_id=1, source_target_pairs={{0,1},{1,0},{2,3},{3,2},{4,5},{5,4},{6,7},{7,6},{8,9},{9,8},{10,11... | collective-permute-start | bytes 884744 | tf_op jit(solution)/shard_map/ppermute | solution.py:121
  38.5 10.5 %collective-permute-start.20 = (bf16[192,384]{1,0:T(8,128)(2,1)}, bf16[192,384]{1,0:T(8,128)(2,1)}, u32[]{:S(2)}, u32[]{:S(2)}) collective-permute-start(bf16[192,384]{1,0:T(8,128)(2,1)} %collective-permute-done.19.refs_7_), channel_id=1, source_target_pairs={{0,4},{4,0},{8,12},{12,8},{1,5},{5,1},{9,13},{13,9},{2,6},{6,2},{1... | collective-permute-start | bytes 442376 | tf_op jit(solution)/shard_map/ppermute | solution.py:121
  38.8 11.3 %collective-permute-start.23 = (bf16[192,384]{1,0:T(8,128)(2,1)}, bf16[192,384]{1,0:T(8,128)(2,1)}, u32[]{:S(2)}, u32[]{:S(2)}) collective-permute-start(bf16[192,384]{1,0:T(8,128)(2,1)} %collective-permute-done.19.refs_7_), channel_id=1, source_target_pairs={{0,16},{16,0},{1,17},{17,1},{2,18},{18,2},{3,19},{19,3},{4,20},{20... | collective-permute-start | bytes 442376 | tf_op jit(solution)/shard_map/ppermute | solution.py:121
  49.0 29.8 %collective-permute-start.25 = (bf16[2,192,768]{2,1,0:T(8,128)(2,1)}, bf16[2,192,768]{2,1,0:T(8,128)(2,1)}, u32[]{:S(2)}, u32[]{:S(2)}) collective-permute-start(bf16[2,192,768]{2,1,0:T(8,128)(2,1)} %get-tuple-element.38), channel_id=1, source_target_pairs={{0,2},{2,0},{1,3},{3,1},{4,6},{6,4},{5,7},{7,5},{8,10},{10,8},{9,1... | collective-permute-start | bytes 1769480 | tf_op jit(solution)/shard_map/ppermute | solution.py:121
  50.1 30.4 %collective-permute-start.26 = (bf16[2,192,768]{2,1,0:T(8,128)(2,1)}, bf16[2,192,768]{2,1,0:T(8,128)(2,1)}, u32[]{:S(2)}, u32[]{:S(2)}) collective-permute-start(bf16[2,192,768]{2,1,0:T(8,128)(2,1)} %get-tuple-element.37), channel_id=1, source_target_pairs={{0,2},{2,0},{1,3},{3,1},{4,6},{6,4},{5,7},{7,5},{8,10},{10,8},{9,1... | collective-permute-start | bytes 1769480 | tf_op jit(solution)/shard_map/ppermute | solution.py:121
  52.0 37.1 %collective-permute-start.29 = (bf16[384,768]{1,0:T(8,128)(2,1)}, bf16[384,768]{1,0:T(8,128)(2,1)S(1)}, u32[]{:S(2)}, u32[]{:S(2)}) collective-permute-start(bf16[384,768]{1,0:T(8,128)(2,1)} %constant_dynamic-slice_fusion), channel_id=1, source_target_pairs={{0,2},{2,0},{1,3},{3,1},{4,6},{6,4},{5,7},{7,5},{8,10},{10,8},{9,1... | collective-permute-start | bytes 1769480 | tf_op jit(solution)/shard_map/ppermute | solution.py:121
  53.0 11.6 %collective-permute-start.21 = (bf16[192,384]{1,0:T(8,128)(2,1)}, bf16[192,384]{1,0:T(8,128)(2,1)S(1)}, u32[]{:S(2)}, u32[]{:S(2)}) collective-permute-start(bf16[192,384]{1,0:T(8,128)(2,1)} %collective-permute-done.18.refs_5_), channel_id=1, source_target_pairs={{0,16},{16,0},{1,17},{17,1},{2,18},{18,2},{3,19},{19,3},{4,20},{20... | collective-permute-start | bytes 442376 | tf_op jit(solution)/shard_map/ppermute | solution.py:121
  54.5 11.4 %collective-permute-start.22 = (bf16[192,384]{1,0:T(8,128)(2,1)}, bf16[192,384]{1,0:T(8,128)(2,1)S(1)}, u32[]{:S(2)}, u32[]{:S(2)}) collective-permute-start(bf16[192,384]{1,0:T(8,128)(2,1)} %collective-permute-done.20.refs_6_), channel_id=1, source_target_pairs={{0,16},{16,0},{1,17},{17,1},{2,18},{18,2},{3,19},{19,3},{4,20},{20... | collective-permute-start | bytes 442376 | tf_op jit(solution)/shard_map/ppermute | solution.py:121
  78.9 29.1 %collective-permute-start.24 = (bf16[224,1536]{1,0:T(8,128)(2,1)}, bf16[224,1536]{1,0:T(8,128)(2,1)S(1)}, u32[]{:S(2)}, u32[]{:S(2)}) collective-permute-start(bf16[224,1536]{1,0:T(8,128)(2,1)} %shard_map.94.mine), channel_id=1, source_target_pairs={{0,1},{1,0},{2,3},{3,2},{4,5},{5,4},{6,7},{7,6},{8,9},{9,8},{10,11... | collective-permute-start | bytes 2064392 | tf_op jit(solution)/shard_map/ppermute | solution.py:121
  78.9 16.5 %collective-permute-start.27 = (bf16[2,192,768]{2,1,0:T(8,128)(2,1)}, bf16[2,192,768]{2,1,0:T(8,128)(2,1)S(1)}, u32[]{:S(2)}, u32[]{:S(2)}) collective-permute-start(bf16[2,192,768]{2,1,0:T(8,128)(2,1)} %collective-permute-done.25.refs_0_), channel_id=1, source_target_pairs={{0,16},{16,0},{1,17},{17,1},{2,18},{18,2},{3,19},{19,3},{4,20},{20... | collective-permute-start | bytes 1769480 | tf_op jit(solution)/shard_map/ppermute | solution.py:121
  80.5 27.5 %collective-permute-start.28 = (bf16[2,192,768]{2,1,0:T(8,128)(2,1)}, bf16[2,192,768]{2,1,0:T(8,128)(2,1)S(1)}, u32[]{:S(2)}, u32[]{:S(2)}) collective-permute-start(bf16[2,192,768]{2,1,0:T(8,128)(2,1)} %collective-permute-done.26.refs_1_), channel_id=1, source_target_pairs={{0,16},{16,0},{1,17},{17,1},{2,18},{18,2},{3,19},{19,3},{4,20},{20... | collective-permute-start | bytes 1769480 | tf_op jit(solution)/shard_map/ppermute | solution.py:121
  89.1 31.0 %collective-permute-start.30 = (bf16[384,768]{1,0:T(8,128)(2,1)S(1)}, bf16[384,768]{1,0:T(8,128)(2,1)S(1)}, u32[]{:S(2)}, u32[]{:S(2)}) collective-permute-start(bf16[384,768]{1,0:T(8,128)(2,1)S(1)} %collective-permute-done.29.refs_0_), channel_id=1, source_target_pairs={{0,16},{16,0},{1,17},{17,1},{2,18},{18,2},{3,19},{19,3},{4,20},{20... | collective-permute-start | bytes 1769480 | tf_op jit(solution)/shard_map/ppermute | solution.py:121
  (27 other events, 252.1 us)
